TPU v7x, 32 devices: a whole 2x2x4 slice. The times are simulated.
32 devices in a mesh: rows: 32 (over z, y, x, core).
Axes of the slice: x: 2, y: 2, z: 4, core: 2. Of those that a mesh axis runs over, the one named last changes fastest.
Arguments:
- diag_noise: bfloat16 [448, 128, 128], P('rows'), may hold values from -1 to 1
- couplings: bfloat16 [448, 3, 128, 128], P('rows'), may hold values from -1 to 1
- shifts: bfloat16 [448, 128], P('rows'), may hold values from 1.5 to 3
- near_devices: int32 [448, 3], P('rows'), may hold values from 0 to 30, all different within a row; in each aligned block of 14 rows (0 to 13, 14 to 27, ...) at most 3 rows name the same one
- near_slots: int32 [448, 3], P('rows'), may hold values from 0 to 13
- vectors: float32 [32, 57344], P(None, 'rows'), may hold values from -6 to 6
Outputs:
- transformed: float32 [32, 57344], P(None, 'rows')
Inputs may be any that keep to these rules, and one draw needn't show every extreme that they name: `near_devices`: each row names three different distances. Among the 14 block rows of one device, no distance is named by more than 3 rows, and in some such group one distance is named by exactly 3 rows.
All inputs are finite; a program needn't handle non-finite values.
Results may differ from a plain program's by a relative error of at most 0.0014.
Values may be sent and summed in bfloat16 or wider, within the bound.
A program may use at most 128 MiB of HBM per device.

v0:
```python
import functools
import math

import jax
import jax.numpy as jnp
from jax import lax
from jax.experimental import pallas as pl
from jax.experimental.pallas import tpu as pltpu
from jax.sharding import PartitionSpec as P

highest = lax.Precision.HIGHEST
PANEL = 16


def split3(x):
    high = x.astype(jnp.bfloat16)
    rest = x - high.astype(jnp.float32)
    mid = rest.astype(jnp.bfloat16)
    low = (rest - mid.astype(jnp.float32)).astype(jnp.bfloat16)
    return high, mid, low


def tdot(a, b):
    return lax.dot_general(
        a, b, (((0,), (0,)), ((), ())), preferred_element_type=jnp.float32
    )


def eliminate(m, pscr, qscr, count, pad, size):
    panel = PANEL
    lane = lax.broadcasted_iota(jnp.int32, (pad, size), 1)
    for block in reversed(range(size // panel)):
        base = block * panel
        rows = [m[pl.ds(base + r, pad, stride=size), :] for r in range(panel)]
        for k in reversed(range(panel)):
            col = base + k
            here = lane == col
            inv = 1.0 / rows[k][:, col : col + 1]
            pivot_row = jnp.where(here, 1.0, rows[k])
            scaled = pivot_row * inv
            for i in range(k):
                f = rows[i][:, col : col + 1]
                rows[i] = jnp.where(here, 0.0, rows[i]) - f * scaled
            if block:
                pscr[pl.ds(k * pad, pad), :] = jnp.where(
                    (lane >= base) & (lane < col), 0.0, pivot_row
                )
                qscr[pl.ds(k * pad, pad), :] = scaled
            m[pl.ds(col, pad, stride=size), :] = jnp.where(
                lane >= col, pivot_row * jnp.sqrt(inv), 0.0
            )
        if block:
            lane_m = lax.broadcasted_iota(jnp.int32, (base, size), 1)
            inside = (lane_m >= base) & (lane_m < base + panel)
            for n in range(count):
                ph, pm, plow = split3(pscr[pl.ds(n, panel, stride=pad), :])
                qh, qm, ql = split3(qscr[pl.ds(n, panel, stride=pad), :])
                right = jnp.concatenate([ph, pm, ph, plow, ph, pm], axis=0)
                left = jnp.concatenate([qh, qh, qm, qh, ql, qm], axis=0)
                update = tdot(left, right)[:base]
                spot = pl.ds(n * size, base)
                m[spot, :] = jnp.where(inside, 0.0, m[spot, :]) - update


def joined(*parts):
    return jnp.concatenate(parts, axis=-1)


def split2(x):
    high = x.astype(jnp.bfloat16)
    return high, (x - high.astype(jnp.float32)).astype(jnp.bfloat16)


def dot_nn(a, b):
    return jnp.dot(a, b, preferred_element_type=jnp.float32)


def dot_nt(a, b):
    return lax.dot_general(
        a, b, (((1,), (1,)), ((), ())), preferred_element_type=jnp.float32
    )


def inverse_kernel(d_ref, e_ref, g_ref, m, pscr, qscr):
    count, size, _ = d_ref.shape
    half = size // 2
    pad = m.shape[0] // size
    for n in range(count):
        m[pl.ds(n * size, size), :] = d_ref[n]
    for n in range(count, pad):
        m[pl.ds(n * size, size), :] = d_ref[0]
    eliminate(m, pscr, qscr, count, pad, size)
    row = lax.broadcasted_iota(jnp.int32, (half, half), 0)
    col = lax.broadcasted_iota(jnp.int32, (half, half), 1)
    row_full = lax.broadcasted_iota(jnp.int32, (size, size), 0)
    col_full = lax.broadcasted_iota(jnp.int32, (size, size), 1)
    for n in range(count):
        h, mid, low = split3(m[pl.ds(n * size, size), :])
        e = tdot(jnp.concatenate([h, h, mid], axis=0), jnp.concatenate([h, mid, h], axis=0))
        left = jnp.where(row >= col, e[:half, :half], e[half:, half:])
        e_ref[n] = joined(left, e[:half, half:]).astype(e_ref.dtype)
        diag = jnp.sum(jnp.where(row_full == col_full, e, 0.0), axis=0, keepdims=True)
        g_ref[n] = jnp.broadcast_to(diag, g_ref.shape[1:]).astype(g_ref.dtype)


def answer_kernel(capacity, served_ref, e_ref, g_ref, out_ref):
    half, size = e_ref.shape[1:]
    tail = g_ref.shape[1]
    row = lax.broadcasted_iota(jnp.int32, (tail, size), 0)

    def step(t, carry):
        tile = jnp.zeros((tail, size), jnp.float32)
        for c in range(capacity):
            source = served_ref[t * capacity + c]
            out_ref[t, pl.ds(c * half, half), :] = e_ref[source]
            tile = jnp.where(row == c, g_ref[source].astype(jnp.float32), tile)
        out_ref[t, pl.ds(capacity * half, tail), :] = tile.astype(out_ref.dtype)
        return carry

    lax.fori_loop(0, out_ref.shape[0], step, 0)


def factor_kernel(
    capacity, scale, target_ref, rank_ref, near_ref, c_ref, d_ref, v_ref,
    k_ref, fh_ref, fl_ref, left_ref, out_ref, m, pscr, qscr,
):
    count, size, _ = d_ref.shape
    half = size // 2
    pad = m.shape[0] // size
    tail = near_ref.shape[1] - capacity * half
    row = lax.broadcasted_iota(jnp.int32, (half, half), 0)
    col = lax.broadcasted_iota(jnp.int32, (half, half), 1)
    tail_row = lax.broadcasted_iota(jnp.int32, (tail, size), 0)

    def schur(n, carry):
        total = d_ref[n]
        for k in range(3):
            t = target_ref[3 * n + k]
            c = rank_ref[3 * n + k]
            packed = near_ref[t, pl.ds(pl.multiple_of(c * half, half), half), :]
            packed = packed.astype(jnp.float32)
            tile = near_ref[t, pl.ds(capacity * half, tail), :].astype(jnp.float32)
            diag = jnp.sum(jnp.where(tail_row == c, tile, 0.0), axis=0, keepdims=True)
            flipped = packed.T
            part = packed[:, :half]
            part_t = flipped[:half, :]
            first = jnp.where(row >= col, part, part_t)
            last = jnp.where(row < col, part, part_t)
            last = jnp.where(row == col, diag[:, half:], last)
            inverse = jnp.concatenate(
                [joined(first, packed[:, half:]), joined(flipped[half:, :], last)], axis=0
            ).astype(jnp.bfloat16)
            coupling = c_ref[n, k]
            f = dot_nn(coupling, inverse) * scale
            high, low = split2(f)
            fh_ref[n, k] = high
            fl_ref[n, k] = low
            total = total - scale * dot_nt(joined(high, low), joined(coupling, coupling))
        m[pl.ds(pl.multiple_of(n * size, size), size), :] = total
        return carry

    lax.fori_loop(0, count, schur, 0, unroll=2)
    for n in range(count, pad):
        m[pl.ds(n * size, size), :] = d_ref[0]
    eliminate(m, pscr, qscr, count, pad, size)
    out_ref[...] = jnp.zeros_like(out_ref)
    for n in range(count):
        k = m[pl.ds(n * size, size), :]
        k_ref[n] = k
        kh, kl = split2(k)
        vh, vl = split2(v_ref[:, n * size : (n + 1) * size])
        left = dot_nn(joined(vh, vh, vl), jnp.concatenate([kh, kl, kh], axis=0))
        left_ref[n] = left
        lh, ll = split2(left)
        for k in range(3):
            r = 3 * n + k
            fh, fl = fh_ref[n, k], fl_ref[n, k]
            sent = dot_nn(joined(lh, lh, ll), jnp.concatenate([fh, fl, fh], axis=0))
            out_ref[target_ref[r] * capacity + rank_ref[r]] = (-sent).astype(out_ref.dtype)


def add_arrived(total, incoming_ref, get, slots):
    count = total.shape[0] - 1
    for s in range(slots):
        wanted = incoming_ref[s]
        spot = jnp.where(wanted < 0, count, wanted)
        total[spot] = total[spot] + get(s).astype(jnp.float32)


def left_kernel(
    capacity, scale, target_ref, rank_ref, incoming_ref, arrived_ref, left_in, c_ref,
    left_ref, out_ref, total,
):
    count = left_in.shape[0]
    slots = arrived_ref.shape[0]
    total[:count] = left_in[...]
    total[count] = jnp.zeros_like(total[count])
    add_arrived(total, incoming_ref, lambda s: arrived_ref[s], slots)
    left_ref[...] = total[:count]
    for s in range(slots):
        spot = s // capacity * 2 * capacity + s % capacity
        out_ref[spot] = total[jnp.maximum(incoming_ref[s], 0)].astype(out_ref.dtype)
        out_ref[spot + capacity] = jnp.zeros_like(out_ref[spot + capacity])
    for n in range(count):
        lh, ll = split2(total[n])
        both = joined(lh, ll)
        for k in range(3):
            r = 3 * n + k
            coupling = c_ref[n, k]
            sent = scale * dot_nn(both, jnp.concatenate([coupling, coupling], axis=0))
            spot = target_ref[r] * (2 * capacity) + capacity + rank_ref[r]
            out_ref[spot] = sent.astype(out_ref.dtype)


def middle_kernel(
    capacity, scale, target_ref, rank_ref, incoming_ref, arrived_ref, own_ref, c_ref,
    middle_ref, out_ref, total,
):
    count = own_ref.shape[0]
    slots = out_ref.shape[0]
    total[count] = jnp.zeros_like(total[count])
    for n in range(count):
        near = own_ref[n]
        for k in range(3):
            r = 3 * n + k
            got = arrived_ref[target_ref[r] * (2 * capacity) + rank_ref[r]]
            near = near + scale * dot_nt(got, c_ref[n, k])
        total[n] = near
    add_arrived(
        total,
        incoming_ref,
        lambda s: arrived_ref[s // capacity * 2 * capacity + capacity + s % capacity],
        slots,
    )
    middle_ref[...] = total[:count]
    for s in range(slots):
        out_ref[s] = total[jnp.maximum(incoming_ref[s], 0)].astype(out_ref.dtype)


def final_kernel(
    capacity, target_ref, rank_ref, arrived_ref, middle_ref, k_ref, fh_ref, fl_ref, out_ref
):
    count, size, _ = k_ref.shape
    for n in range(count):
        part = middle_ref[n]
        for k in range(3):
            r = 3 * n + k
            got = arrived_ref[target_ref[r] * capacity + rank_ref[r]]
            part = part - dot_nt(joined(got, got), joined(fh_ref[n, k], fl_ref[n, k]))
        ph, plow = split2(part)
        kh, kl = split2(k_ref[n])
        out_ref[:, n * size : (n + 1) * size] = dot_nt(
            joined(ph, ph, plow), joined(kh, kl, kh)
        )


def call(kernel, scalars, arrays, shapes, scratch=()):
    smem = pl.BlockSpec(memory_space=pltpu.SMEM)
    vmem = pl.BlockSpec(memory_space=pltpu.VMEM)
    return pl.pallas_call(
        kernel,
        out_shape=[jax.ShapeDtypeStruct(shape, dtype) for shape, dtype in shapes],
        in_specs=[smem] * len(scalars) + [vmem] * len(arrays),
        out_specs=[vmem] * len(shapes),
        scratch_shapes=[pltpu.VMEM(shape, jnp.float32) for shape in scratch],
    )(*scalars, *arrays)


def build_diag(noise_block, shift_block, factor):
    noise_block = noise_block.astype(jnp.float32) * factor
    symmetric = (noise_block + jnp.swapaxes(noise_block, -1, -2)) * 0.5
    eye_block = jnp.eye(noise_block.shape[-1], dtype=jnp.float32)
    return symmetric + shift_block.astype(jnp.float32)[..., :, None] * eye_block


def exchange(x, dev_count):
    shape = x.shape
    x = x.reshape(dev_count, -1, *shape[1:])
    x = lax.all_to_all(x, "rows", split_axis=0, concat_axis=0, tiled=True)
    return x.reshape(shape)


def body(diag_noise, couplings, shifts, near_devices, near_slots, vectors):
    dev_count = lax.axis_size("rows")
    my_index = lax.axis_index("rows")
    row_count = diag_noise.shape[0]
    block_size = diag_noise.shape[1]
    vec_count = vectors.shape[0]
    capacity = 3 * row_count // (dev_count - 1) + 2
    slot_total = dev_count * capacity
    factor = 0.5 / math.sqrt(block_size)
    coupling_factor = 0.4 / math.sqrt(block_size)
    target = ((my_index - 1 - near_devices) % dev_count).reshape(-1)
    device_onehot = (target[:, None] == jnp.arange(dev_count, dtype=jnp.int32)[None, :]).astype(
        jnp.int32
    )
    running = jnp.cumsum(device_onehot, axis=0) - 1
    rank = jnp.sum(running * device_onehot, axis=1)
    position = target * capacity + rank
    hit = position[None, :] == jnp.arange(slot_total, dtype=jnp.int32)[:, None]
    asked_slots = jnp.sum(jnp.where(hit, near_slots.reshape(1, -1) + 1, 0), axis=1) - 1
    incoming = exchange(asked_slots, dev_count)
    served = jnp.maximum(incoming, 0)
    diag_own = build_diag(diag_noise, shifts, factor)

    bf16, f32 = jnp.bfloat16, jnp.float32
    half = block_size // 2
    tail = 16
    pad = -(-row_count // 8) * 8
    work = ((pad * block_size, block_size),) + ((PANEL * pad, block_size),) * 2
    packed, diags = call(
        inverse_kernel,
        (),
        (diag_own,),
        (((row_count, half, block_size), bf16), ((row_count, tail, block_size), bf16)),
        work,
    )
    (answer,) = call(
        functools.partial(answer_kernel, capacity),
        (served,),
        (packed, diags),
        (((dev_count, capacity * half + tail, block_size), bf16),),
    )
    near = exchange(answer, dev_count)
    rows_shape = (row_count, vec_count, block_size)
    total_shape = ((row_count + 1, vec_count, block_size),)
    slots_shape = (slot_total, vec_count, block_size)
    f_shape = (row_count, 3, block_size, block_size)
    k_all, f_high, f_low, left, outgoing = call(
        functools.partial(factor_kernel, capacity, coupling_factor),
        (target, rank),
        (near, couplings, diag_own, vectors),
        (
            ((row_count, block_size, block_size), f32),
            (f_shape, bf16),
            (f_shape, bf16),
            (rows_shape, f32),
            (slots_shape, bf16),
        ),
        work,
    )
    arrived = exchange(outgoing, dev_count)
    left, outgoing = call(
        functools.partial(left_kernel, capacity, coupling_factor),
        (target, rank, incoming),
        (arrived, left, couplings),
        ((rows_shape, f32), ((2 * slot_total, vec_count, block_size), bf16)),
        total_shape,
    )
    arrived = exchange(outgoing, dev_count)
    own = jnp.einsum("rva,rab->rvb", left, diag_own, precision=highest)
    middle, outgoing = call(
        functools.partial(middle_kernel, capacity, coupling_factor),
        (target, rank, incoming),
        (arrived, own, couplings),
        ((rows_shape, f32), (slots_shape, bf16)),
        total_shape,
    )
    arrived = exchange(outgoing, dev_count)
    (result,) = call(
        functools.partial(final_kernel, capacity),
        (target, rank),
        (arrived, middle, k_all, f_high, f_low),
        ((vectors.shape, f32),),
    )
    return result


def solution(mesh):
    return jax.shard_map(
        body,
        mesh=mesh,
        in_specs=(
            P("rows", None, None),
            P("rows", None, None, None),
            P("rows", None),
            P("rows", None),
            P("rows", None),
            P(None, "rows"),
        ),
        out_specs=P(None, "rows"),
        check_vma=False,
    )
```

profile of v0, /device:TPU:0, one launch (start us, length us, event | category | flops | bytes accessed | tf_op | source)
XLA Modules:
  0.0 214.3 jit_solution(84472464402985456)
XLA Ops:
  0.0 0.7 broadcast_add_fusion
  0.9 0.7 add_select_fusion
  2.2 0.7 sub.24
  2.9 7.3 %all-to-all-start = ((s32[32,1,3]{2,1,0:T(1,128)}), s32[32,1,3]{2,1,0:T(1,128)S(1)}, u32[]{:S(2)}, u32[]{:S(2)}) async-start(s32[32,1,3]{2,1,0:T(1,128)} %bitcast), calls=%async_computation | async-start | bytes 32768 | tf_op jit(solution)/shard_map/all_to_all | solution.py:279
  10.3 0.7 convert_element_type.18
  11.0 1.3 copy.24
  12.4 0.3 copy.25
  12.7 1.2 fusion.1.d_ref
  13.9 18.1 %shard_map.64 = (bf16[14,64,128]{2,1,0:T(8,128)(2,1)}, bf16[14,16,128]{2,1,0:T(8,128)(2,1)}) custom-call(f32[14,128,128]{2,1,0:T(8,128)} %fusion.1.d_ref), custom_call_target="tpu_custom_call" | custom-call | tf_op jit(solution)/shard_map/pallas_call | solution.py:260
  32.0 0.5 broadcast.48
  32.5 0.7 reduce.3
  33.3 0.5 broadcast_maximum_fusion.served_ref
  33.8 2.5 %shard_map.65 = bf16[32,208,128]{2,1,0:T(8,128)(2,1)} custom-call(s32[96]{0:T(128)} %broadcast_maximum_fusion.served_ref, bf16[14,64,128]{2,1,0:T(8,128)(2,1)} %get-tuple-element.16.e_ref, bf16[14,16,128]{2,1,0:T(8,128)(2,1)} %get-tuple-element.17.g_ref), custom_call_target="tpu_custom_call" | custom-call | tf_op jit(solution)/shard_map/pallas_call | solution.py:260
  36.4 46.4 %all_to_all.26 = bf16[32,1,208,128]{3,2,1,0:T(8,128)(2,1)} all-to-all(bf16[32,1,208,128]{3,2,1,0:T(8,128)(2,1)} %bitcast.20), channel_id=1, replica_groups=mesh['rows'=32] {'rows'}, dimensions={0} | all-to-all | bytes 3407872 | tf_op jit(solution)/shard_map/all_to_all | solution.py:279
  82.8 26.3 %shard_map.66 = (f32[14,128,128]{2,1,0:T(8,128)}, bf16[14,3,128,128]{3,2,1,0:T(8,128)(2,1)}, bf16[14,3,128,128]{3,2,1,0:T(8,128)(2,1)}, f32[14,32,128]{2,1,0:T(8,128)}, bf16[96,32,128]{2,1,0:T(8,128)(2,1)}) custom-call(s32[42]{0:T(128)} %copy-done.3, s32[42]{0:T(128)} %copy-done.4, bf16[32,208,128]{2,1,0:T(8,128)(2,1)} %bitcast.19, ...), custom_call_target="tpu_custom_call" | custom-call | tf_op jit(solution)/shard_map/pallas_call | solution.py:260
  109.1 24.1 %all_to_all.27 = bf16[32,3,32,128]{3,2,1,0:T(8,128)(2,1)} all-to-all(bf16[32,3,32,128]{3,2,1,0:T(8,128)(2,1)} %bitcast.25), channel_id=1, replica_groups=mesh['rows'=32] {'rows'}, dimensions={0} | all-to-all | bytes 1572864 | tf_op jit(solution)/shard_map/all_to_all | solution.py:279
  133.2 4.0 %shard_map.67 = (f32[14,32,128]{2,1,0:T(8,128)}, bf16[192,32,128]{2,1,0:T(8,128)(2,1)}) custom-call(s32[42]{0:T(128)} %copy-done.3, s32[42]{0:T(128)} %copy-done.4, s32[96]{0:T(128)} %copy-done.5, bf16[96,32,128]{2,1,0:T(8,128)(2,1)} %bitcast.22, f32[14,32,128]{2,1,0:T(8,128)} %get-tuple-element.19.left_in, bf16[14,3,128,128]{3,2,1,0:T(8,128)(2,1)} %c_ref.5), custom_call_target="tpu_custom_call" | custom-call | tf_op jit(solution)/shard_map/pallas_call | solution.py:260
  137.2 3.9 %all-to-all-start.3 = ((bf16[32,6,32,128]{3,2,1,0:T(8,128)(2,1)}), bf16[32,6,32,128]{3,2,1,0:T(8,128)(2,1)S(1)}, u32[]{:S(2)}, u32[]{:S(2)}) async-start(bf16[32,6,32,128]{3,2,1,0:T(8,128)(2,1)} %bitcast.24), calls=%async_computation.3 | async-start | bytes 3145728 | tf_op jit(solution)/shard_map/all_to_all | solution.py:279
  141.1 1.6 fusion.5.own_ref
  142.6 35.9 %all-to-all-done.3 = bf16[32,6,32,128]{3,2,1,0:T(8,128)(2,1)S(1)} async-done(((bf16[32,6,32,128]{3,2,1,0:T(8,128)(2,1)}), bf16[32,6,32,128]{3,2,1,0:T(8,128)(2,1)S(1)}, u32[]{:S(2)}, u32[]{:S(2)}) %all-to-all-start.3) | async-done | bytes 1572896 | tf_op jit(solution)/shard_map/all_to_all | solution.py:279
  178.5 1.2 copy-done.1
  179.7 4.3 %shard_map.68 = (f32[14,32,128]{2,1,0:T(8,128)}, bf16[96,32,128]{2,1,0:T(8,128)(2,1)}) custom-call(s32[42]{0:T(128)} %copy-done.3, s32[42]{0:T(128)} %copy-done.4, s32[96]{0:T(128)} %copy-done.5, bf16[192,32,128]{2,1,0:T(8,128)(2,1)} %bitcast.21, f32[14,32,128]{2,1,0:T(8,128)} %fusion.5.own_ref, bf16[14,3,128,128]{3,2,1,0:T(8,128)(2,1)} %c_ref.5), custom_call_target="tpu_custom_call" | custom-call | tf_op jit(solution)/shard_map/pallas_call | solution.py:260
  184.0 24.4 %all_to_all.28 = bf16[32,3,32,128]{3,2,1,0:T(8,128)(2,1)} all-to-all(bf16[32,3,32,128]{3,2,1,0:T(8,128)(2,1)} %bitcast.26), channel_id=1, replica_groups=mesh['rows'=32] {'rows'}, dimensions={0} | all-to-all | bytes 1572864 | tf_op jit(solution)/shard_map/all_to_all | solution.py:279
  208.5 5.9 %shard_map.69 = f32[32,1792]{1,0:T(8,128)} custom-call(s32[42]{0:T(128)} %copy-done.3, s32[42]{0:T(128)} %copy-done.4, bf16[96,32,128]{2,1,0:T(8,128)(2,1)} %bitcast.23, f32[14,32,128]{2,1,0:T(8,128)} %get-tuple-element.23.middle_ref, f32[14,128,128]{2,1,0:T(8,128)} %get-tuple-element.24.k_ref, bf16[14,3,128,128]{3,2,1,0:T(8,128)(2,1)} %get-tuple-element.25.fh_ref, ...), custom_call_target="tpu_custom_call" | custom-call | tf_op jit(solution)/shard_map/pallas_call | solution.py:260
  (25 shorter events, 1.0 us)
Async XLA Ops:
  1.8 10.9 %copy-start.3 = (s32[42]{0:T(128)}, s32[42]{0:T(128)S(1)}, u32[]{:S(2)}) copy-start(s32[42]{0:T(128)S(1)} %reshape.75.target_ref) | copy-start | bytes 508
  2.1 10.6 %copy-start.4 = (s32[42]{0:T(128)}, s32[42]{0:T(128)S(1)}, u32[]{:S(2)}) copy-start(s32[42]{0:T(128)S(1)} %select_reduce_fusion.1.rank_ref) | copy-start | bytes 508
  2.9 29.1 %all-to-all-start = ((s32[32,1,3]{2,1,0:T(1,128)}), s32[32,1,3]{2,1,0:T(1,128)S(1)}, u32[]{:S(2)}, u32[]{:S(2)}) async-start(s32[32,1,3]{2,1,0:T(1,128)} %bitcast), calls=%async_computation | async-start | bytes 32768 | tf_op jit(solution)/shard_map/all_to_all | solution.py:279
  33.3 49.5 %copy-start.5 = (s32[96]{0:T(128)}, s32[96]{0:T(128)S(1)}, u32[]{:S(2)}) copy-start(s32[96]{0:T(128)S(1)} %reshape.76.incoming_ref) | copy-start | bytes 1156
  137.2 3.9 %copy-start = (f32[14,128,128]{2,1,0:T(8,128)S(1)}, f32[14,128,128]{2,1,0:T(8,128)}, u32[]{:S(2)}) copy-start(f32[14,128,128]{2,1,0:T(8,128)} %fusion.1.d_ref) | copy-start | bytes 2752516
  137.2 3.9 %copy-start.2 = (f32[14,32,128]{2,1,0:T(8,128)S(1)}, f32[14,32,128]{2,1,0:T(8,128)}, u32[]{:S(2)}) copy-start(f32[14,32,128]{2,1,0:T(8,128)} %get-tuple-element.21) | copy-start | bytes 688132
  137.2 41.3 %all-to-all-start.3 = ((bf16[32,6,32,128]{3,2,1,0:T(8,128)(2,1)}), bf16[32,6,32,128]{3,2,1,0:T(8,128)(2,1)S(1)}, u32[]{:S(2)}, u32[]{:S(2)}) async-start(bf16[32,6,32,128]{3,2,1,0:T(8,128)(2,1)} %bitcast.24), calls=%async_computation.3 | async-start | bytes 3145728 | tf_op jit(solution)/shard_map/all_to_all | solution.py:279
  178.5 1.2 copy-start.1
where the time goes:
time: 215 us; the launch traced here: 214 us
  blocking collectives  95 us (44%)
  Pallas kernels  61.1 us (28%)
  waiting for transfers between devices  35.9 us (17%)
  starting transfers between devices  11.2 us (5%)
  other arithmetic  5.01 us (2%)
  local copies, waits for them, and re-layouts  4.48 us (2%)
    all_to_all x3, blocking collectives, exchange(): x = lax.all_to_all(x, 'rows', split_axis=0, concat_axis=0, tiled=True)  95 us
    pallas_call x6, Pallas kernels, call(): pl.pallas_call(kernel, out_shape=[jax.ShapeDtypeStruct(shape, dtype) for...  61.1 us
    all_to_all x2, waiting for transfers between devices, exchange(): x = lax.all_to_all(x, 'rows', split_axis=0, concat_axis=0, tiled=True)  35.9 us
    all_to_all x2, starting transfers between devices, exchange(): x = lax.all_to_all(x, 'rows', split_axis=0, concat_axis=0, tiled=True)  11.2 us
  transfers between devices with their start and end apart: 2, of which 1 were waited for; matrix products, arithmetic and copies ran while one was open for 2% of the time, Pallas kernels for 8%

commit v1 on v0

--- a/solution.py
+++ b/solution.py
@@ -10,6 +10,7 @@
 
 highest = lax.Precision.HIGHEST
 PANEL = 16
+GROUP = 4
 
 
 def split3(x):
@@ -35,12 +36,22 @@
         for k in reversed(range(panel)):
             col = base + k
             here = lane == col
-            inv = 1.0 / rows[k][:, col : col + 1]
+            if (k + 1) % GROUP == 0:
+                first = k + 1 - GROUP
+                tile = {
+                    (i, c): jnp.broadcast_to(rows[i][:, base + c : base + c + 1], (pad, size))
+                    for c in range(first, k + 1)
+                    for i in range(c + 1)
+                }
+            inv = 1.0 / tile[k, k]
+            for c in reversed(range(first, k)):
+                ratio = tile[c, k] * inv
+                for i in range(c + 1):
+                    tile[i, c] = tile[i, c] - tile[i, k] * ratio
             pivot_row = jnp.where(here, 1.0, rows[k])
             scaled = pivot_row * inv
             for i in range(k):
-                f = rows[i][:, col : col + 1]
-                rows[i] = jnp.where(here, 0.0, rows[i]) - f * scaled
+                rows[i] = jnp.where(here, 0.0, rows[i]) - tile[i, k] * scaled
             if block:
                 pscr[pl.ds(k * pad, pad), :] = jnp.where(
                     (lane >= base) & (lane < col), 0.0, pivot_row

time: 215 us -> 202 us (0.940)
  Pallas kernels: 61.1 us -> 48 us
    pallas_call x6, Pallas kernels: 61.1 us -> 48 us  [call(): pl.pallas_call(kernel, out_shape=[jax.ShapeDtypeStruct(shape, dtype) for...]
  transfers between devices with their start and end apart: 2 -> 2, of which waited for: 1 -> 1; matrix products, arithmetic and copies ran while one was open for 2% -> 3% of each run, Pallas kernels for 8% -> 5%
where the time goes in v1:
time: 202 us; the launch traced here: 201 us
  blocking collectives  95 us (47%)
  Pallas kernels  48 us (24%)
  waiting for transfers between devices  35.9 us (18%)
  starting transfers between devices  11.2 us (6%)
  other arithmetic  5.01 us (2%)
  local copies, waits for them, and re-layouts  4.48 us (2%)
    all_to_all x3, blocking collectives, exchange(): x = lax.all_to_all(x, 'rows', split_axis=0, concat_axis=0, tiled=True)  95 us
    pallas_call x6, Pallas kernels, call(): pl.pallas_call(kernel, out_shape=[jax.ShapeDtypeStruct(shape, dtype) for...  48 us
    all_to_all x2, waiting for transfers between devices, exchange(): x = lax.all_to_all(x, 'rows', split_axis=0, concat_axis=0, tiled=True)  35.9 us
    all_to_all x2, starting transfers between devices, exchange(): x = lax.all_to_all(x, 'rows', split_axis=0, concat_axis=0, tiled=True)  11.2 us
  transfers between devices with their start and end apart: 2, of which 1 were waited for; matrix products, arithmetic and copies ran while one was open for 3% of the time, Pallas kernels for 5%

profile of v1, /device:TPU:0, one launch (start us, length us, event | category | flops | bytes accessed | tf_op | source)
XLA Modules:
  0.0 201.2 jit_solution(7006590586585981063)
XLA Ops:
  0.0 0.7 broadcast_add_fusion
  0.9 0.7 add_select_fusion
  2.2 0.7 sub.24
  2.9 7.3 %all-to-all-start = ((s32[32,1,3]{2,1,0:T(1,128)}), s32[32,1,3]{2,1,0:T(1,128)S(1)}, u32[]{:S(2)}, u32[]{:S(2)}) async-start(s32[32,1,3]{2,1,0:T(1,128)} %bitcast), calls=%async_computation | async-start | bytes 32768 | tf_op jit(solution)/shard_map/all_to_all | solution.py:290
  10.3 0.7 convert_element_type.18
  11.0 1.3 copy.24
  12.4 0.3 copy.25
  12.7 1.2 fusion.1.d_ref
  13.9 9.5 %shard_map.64 = (bf16[14,64,128]{2,1,0:T(8,128)(2,1)}, bf16[14,16,128]{2,1,0:T(8,128)(2,1)}) custom-call(f32[14,128,128]{2,1,0:T(8,128)} %fusion.1.d_ref), custom_call_target="tpu_custom_call" | custom-call | tf_op jit(solution)/shard_map/pallas_call | solution.py:271
  23.4 0.5 broadcast.48
  23.9 0.7 reduce.3
  24.7 0.5 broadcast_maximum_fusion.served_ref
  25.3 2.5 %shard_map.65 = bf16[32,208,128]{2,1,0:T(8,128)(2,1)} custom-call(s32[96]{0:T(128)} %broadcast_maximum_fusion.served_ref, bf16[14,64,128]{2,1,0:T(8,128)(2,1)} %get-tuple-element.16.e_ref, bf16[14,16,128]{2,1,0:T(8,128)(2,1)} %get-tuple-element.17.g_ref), custom_call_target="tpu_custom_call" | custom-call | tf_op jit(solution)/shard_map/pallas_call | solution.py:271
  27.8 46.4 %all_to_all.26 = bf16[32,1,208,128]{3,2,1,0:T(8,128)(2,1)} all-to-all(bf16[32,1,208,128]{3,2,1,0:T(8,128)(2,1)} %bitcast.20), channel_id=1, replica_groups=mesh['rows'=32] {'rows'}, dimensions={0} | all-to-all | bytes 3407872 | tf_op jit(solution)/shard_map/all_to_all | solution.py:290
  74.2 21.8 %shard_map.66 = (f32[14,128,128]{2,1,0:T(8,128)}, bf16[14,3,128,128]{3,2,1,0:T(8,128)(2,1)}, bf16[14,3,128,128]{3,2,1,0:T(8,128)(2,1)}, f32[14,32,128]{2,1,0:T(8,128)}, bf16[96,32,128]{2,1,0:T(8,128)(2,1)}) custom-call(s32[42]{0:T(128)} %copy-done.3, s32[42]{0:T(128)} %copy-done.4, bf16[32,208,128]{2,1,0:T(8,128)(2,1)} %bitcast.19, ...), custom_call_target="tpu_custom_call" | custom-call | tf_op jit(solution)/shard_map/pallas_call | solution.py:271
  96.0 24.1 %all_to_all.27 = bf16[32,3,32,128]{3,2,1,0:T(8,128)(2,1)} all-to-all(bf16[32,3,32,128]{3,2,1,0:T(8,128)(2,1)} %bitcast.25), channel_id=1, replica_groups=mesh['rows'=32] {'rows'}, dimensions={0} | all-to-all | bytes 1572864 | tf_op jit(solution)/shard_map/all_to_all | solution.py:290
  120.1 4.0 %shard_map.67 = (f32[14,32,128]{2,1,0:T(8,128)}, bf16[192,32,128]{2,1,0:T(8,128)(2,1)}) custom-call(s32[42]{0:T(128)} %copy-done.3, s32[42]{0:T(128)} %copy-done.4, s32[96]{0:T(128)} %copy-done.5, bf16[96,32,128]{2,1,0:T(8,128)(2,1)} %bitcast.22, f32[14,32,128]{2,1,0:T(8,128)} %get-tuple-element.19.left_in, bf16[14,3,128,128]{3,2,1,0:T(8,128)(2,1)} %c_ref.5), custom_call_target="tpu_custom_call" | custom-call | tf_op jit(solution)/shard_map/pallas_call | solution.py:271
  124.1 3.8 %all-to-all-start.3 = ((bf16[32,6,32,128]{3,2,1,0:T(8,128)(2,1)}), bf16[32,6,32,128]{3,2,1,0:T(8,128)(2,1)S(1)}, u32[]{:S(2)}, u32[]{:S(2)}) async-start(bf16[32,6,32,128]{3,2,1,0:T(8,128)(2,1)} %bitcast.24), calls=%async_computation.3 | async-start | bytes 3145728 | tf_op jit(solution)/shard_map/all_to_all | solution.py:290
  127.9 1.6 fusion.5.own_ref
  129.5 35.9 %all-to-all-done.3 = bf16[32,6,32,128]{3,2,1,0:T(8,128)(2,1)S(1)} async-done(((bf16[32,6,32,128]{3,2,1,0:T(8,128)(2,1)}), bf16[32,6,32,128]{3,2,1,0:T(8,128)(2,1)S(1)}, u32[]{:S(2)}, u32[]{:S(2)}) %all-to-all-start.3) | async-done | bytes 1572896 | tf_op jit(solution)/shard_map/all_to_all | solution.py:290
  165.4 1.2 copy-done.1
  166.6 4.3 %shard_map.68 = (f32[14,32,128]{2,1,0:T(8,128)}, bf16[96,32,128]{2,1,0:T(8,128)(2,1)}) custom-call(s32[42]{0:T(128)} %copy-done.3, s32[42]{0:T(128)} %copy-done.4, s32[96]{0:T(128)} %copy-done.5, bf16[192,32,128]{2,1,0:T(8,128)(2,1)} %bitcast.21, f32[14,32,128]{2,1,0:T(8,128)} %fusion.5.own_ref, bf16[14,3,128,128]{3,2,1,0:T(8,128)(2,1)} %c_ref.5), custom_call_target="tpu_custom_call" | custom-call | tf_op jit(solution)/shard_map/pallas_call | solution.py:271
  170.9 24.4 %all_to_all.28 = bf16[32,3,32,128]{3,2,1,0:T(8,128)(2,1)} all-to-all(bf16[32,3,32,128]{3,2,1,0:T(8,128)(2,1)} %bitcast.26), channel_id=1, replica_groups=mesh['rows'=32] {'rows'}, dimensions={0} | all-to-all | bytes 1572864 | tf_op jit(solution)/shard_map/all_to_all | solution.py:290
  195.3 5.9 %shard_map.69 = f32[32,1792]{1,0:T(8,128)} custom-call(s32[42]{0:T(128)} %copy-done.3, s32[42]{0:T(128)} %copy-done.4, bf16[96,32,128]{2,1,0:T(8,128)(2,1)} %bitcast.23, f32[14,32,128]{2,1,0:T(8,128)} %get-tuple-element.23.middle_ref, f32[14,128,128]{2,1,0:T(8,128)} %get-tuple-element.24.k_ref, bf16[14,3,128,128]{3,2,1,0:T(8,128)(2,1)} %get-tuple-element.25.fh_ref, ...), custom_call_target="tpu_custom_call" | custom-call | tf_op jit(solution)/shard_map/pallas_call | solution.py:271
  (25 shorter events, 1.0 us)
Async XLA Ops:
  1.8 10.9 %copy-start.3 = (s32[42]{0:T(128)}, s32[42]{0:T(128)S(1)}, u32[]{:S(2)}) copy-start(s32[42]{0:T(128)S(1)} %reshape.75.target_ref) | copy-start | bytes 508
  2.1 10.6 %copy-start.4 = (s32[42]{0:T(128)}, s32[42]{0:T(128)S(1)}, u32[]{:S(2)}) copy-start(s32[42]{0:T(128)S(1)} %select_reduce_fusion.1.rank_ref) | copy-start | bytes 508
  2.9 20.5 %all-to-all-start = ((s32[32,1,3]{2,1,0:T(1,128)}), s32[32,1,3]{2,1,0:T(1,128)S(1)}, u32[]{:S(2)}, u32[]{:S(2)}) async-start(s32[32,1,3]{2,1,0:T(1,128)} %bitcast), calls=%async_computation | async-start | bytes 32768 | tf_op jit(solution)/shard_map/all_to_all | solution.py:290
  24.7 49.5 %copy-start.5 = (s32[96]{0:T(128)}, s32[96]{0:T(128)S(1)}, u32[]{:S(2)}) copy-start(s32[96]{0:T(128)S(1)} %reshape.76.incoming_ref) | copy-start | bytes 1156
  124.1 3.9 %copy-start = (f32[14,128,128]{2,1,0:T(8,128)S(1)}, f32[14,128,128]{2,1,0:T(8,128)}, u32[]{:S(2)}) copy-start(f32[14,128,128]{2,1,0:T(8,128)} %fusion.1.d_ref) | copy-start | bytes 2752516
  124.1 3.9 %copy-start.2 = (f32[14,32,128]{2,1,0:T(8,128)S(1)}, f32[14,32,128]{2,1,0:T(8,128)}, u32[]{:S(2)}) copy-start(f32[14,32,128]{2,1,0:T(8,128)} %get-tuple-element.21) | copy-start | bytes 688132
  124.1 41.3 %all-to-all-start.3 = ((bf16[32,6,32,128]{3,2,1,0:T(8,128)(2,1)}), bf16[32,6,32,128]{3,2,1,0:T(8,128)(2,1)S(1)}, u32[]{:S(2)}, u32[]{:S(2)}) async-start(bf16[32,6,32,128]{3,2,1,0:T(8,128)(2,1)} %bitcast.24), calls=%async_computation.3 | async-start | bytes 3145728 | tf_op jit(solution)/shard_map/all_to_all | solution.py:290
  165.4 1.2 copy-start.1

commit v2 on v1

--- a/solution.py
+++ b/solution.py
@@ -128,7 +128,7 @@
         out_ref[t, pl.ds(capacity * half, tail), :] = tile.astype(out_ref.dtype)
         return carry
 
-    lax.fori_loop(0, out_ref.shape[0], step, 0)
+    lax.fori_loop(0, out_ref.shape[0], step, 0, unroll=8)
 
 
 def factor_kernel(
@@ -170,7 +170,7 @@
         m[pl.ds(pl.multiple_of(n * size, size), size), :] = total
         return carry
 
-    lax.fori_loop(0, count, schur, 0, unroll=2)
+    lax.fori_loop(0, count, schur, 0, unroll=7)
     for n in range(count, pad):
         m[pl.ds(n * size, size), :] = d_ref[0]
     eliminate(m, pscr, qscr, count, pad, size)

time: 202 us -> 201 us (level)
  no operation moved by 1% of the time
where the time goes in v2:
time: 201 us; the launch traced here: 200 us
  blocking collectives  95 us (47%)
  Pallas kernels  46.6 us (23%)
  waiting for transfers between devices  35.9 us (18%)
  starting transfers between devices  11.2 us (6%)
  other arithmetic  5.01 us (2%)
  local copies, waits for them, and re-layouts  4.48 us (2%)
    all_to_all x3, blocking collectives, exchange(): x = lax.all_to_all(x, 'rows', split_axis=0, concat_axis=0, tiled=True)  95 us
    pallas_call x6, Pallas kernels, call(): pl.pallas_call(kernel, out_shape=[jax.ShapeDtypeStruct(shape, dtype) for...  46.6 us
    all_to_all x2, waiting for transfers between devices, exchange(): x = lax.all_to_all(x, 'rows', split_axis=0, concat_axis=0, tiled=True)  35.9 us
    all_to_all x2, starting transfers between devices, exchange(): x = lax.all_to_all(x, 'rows', split_axis=0, concat_axis=0, tiled=True)  11.2 us
  transfers between devices with their start and end apart: 2, of which 1 were waited for; matrix products, arithmetic and copies ran while one was open for 3% of the time, Pallas kernels for 5%

profile of v2, /device:TPU:0, one launch (start us, length us, event | category | flops | bytes accessed | tf_op | source)
XLA Modules:
  0.0 199.9 jit_solution(11885102189549999676)
XLA Ops:
  0.0 0.7 broadcast_add_fusion
  0.9 0.7 add_select_fusion
  2.2 0.7 sub.24
  2.9 7.3 %all-to-all-start = ((s32[32,1,3]{2,1,0:T(1,128)}), s32[32,1,3]{2,1,0:T(1,128)S(1)}, u32[]{:S(2)}, u32[]{:S(2)}) async-start(s32[32,1,3]{2,1,0:T(1,128)} %bitcast), calls=%async_computation | async-start | bytes 32768 | tf_op jit(solution)/shard_map/all_to_all | solution.py:290
  10.3 0.7 convert_element_type.18
  11.0 1.3 copy.24
  12.4 0.3 copy.25
  12.7 1.2 fusion.1.d_ref
  13.9 9.5 %shard_map.64 = (bf16[14,64,128]{2,1,0:T(8,128)(2,1)}, bf16[14,16,128]{2,1,0:T(8,128)(2,1)}) custom-call(f32[14,128,128]{2,1,0:T(8,128)} %fusion.1.d_ref), custom_call_target="tpu_custom_call" | custom-call | tf_op jit(solution)/shard_map/pallas_call | solution.py:271
  23.4 0.5 broadcast.48
  23.9 0.7 reduce.3
  24.7 0.5 broadcast_maximum_fusion.served_ref
  25.3 2.3 %shard_map.65 = bf16[32,208,128]{2,1,0:T(8,128)(2,1)} custom-call(s32[96]{0:T(128)} %broadcast_maximum_fusion.served_ref, bf16[14,64,128]{2,1,0:T(8,128)(2,1)} %get-tuple-element.16.e_ref, bf16[14,16,128]{2,1,0:T(8,128)(2,1)} %get-tuple-element.17.g_ref), custom_call_target="tpu_custom_call" | custom-call | tf_op jit(solution)/shard_map/pallas_call | solution.py:271
  27.6 46.4 %all_to_all.26 = bf16[32,1,208,128]{3,2,1,0:T(8,128)(2,1)} all-to-all(bf16[32,1,208,128]{3,2,1,0:T(8,128)(2,1)} %bitcast.20), channel_id=1, replica_groups=mesh['rows'=32] {'rows'}, dimensions={0} | all-to-all | bytes 3407872 | tf_op jit(solution)/shard_map/all_to_all | solution.py:290
  74.0 20.6 %shard_map.66 = (f32[14,128,128]{2,1,0:T(8,128)}, bf16[14,3,128,128]{3,2,1,0:T(8,128)(2,1)}, bf16[14,3,128,128]{3,2,1,0:T(8,128)(2,1)}, f32[14,32,128]{2,1,0:T(8,128)}, bf16[96,32,128]{2,1,0:T(8,128)(2,1)}) custom-call(s32[42]{0:T(128)} %copy-done.3, s32[42]{0:T(128)} %copy-done.4, bf16[32,208,128]{2,1,0:T(8,128)(2,1)} %bitcast.19, ...), custom_call_target="tpu_custom_call" | custom-call | tf_op jit(solution)/shard_map/pallas_call | solution.py:271
  94.6 24.1 %all_to_all.27 = bf16[32,3,32,128]{3,2,1,0:T(8,128)(2,1)} all-to-all(bf16[32,3,32,128]{3,2,1,0:T(8,128)(2,1)} %bitcast.25), channel_id=1, replica_groups=mesh['rows'=32] {'rows'}, dimensions={0} | all-to-all | bytes 1572864 | tf_op jit(solution)/shard_map/all_to_all | solution.py:290
  118.7 4.0 %shard_map.67 = (f32[14,32,128]{2,1,0:T(8,128)}, bf16[192,32,128]{2,1,0:T(8,128)(2,1)}) custom-call(s32[42]{0:T(128)} %copy-done.3, s32[42]{0:T(128)} %copy-done.4, s32[96]{0:T(128)} %copy-done.5, bf16[96,32,128]{2,1,0:T(8,128)(2,1)} %bitcast.22, f32[14,32,128]{2,1,0:T(8,128)} %get-tuple-element.19.left_in, bf16[14,3,128,128]{3,2,1,0:T(8,128)(2,1)} %c_ref.5), custom_call_target="tpu_custom_call" | custom-call | tf_op jit(solution)/shard_map/pallas_call | solution.py:271
  122.7 3.8 %all-to-all-start.3 = ((bf16[32,6,32,128]{3,2,1,0:T(8,128)(2,1)}), bf16[32,6,32,128]{3,2,1,0:T(8,128)(2,1)S(1)}, u32[]{:S(2)}, u32[]{:S(2)}) async-start(bf16[32,6,32,128]{3,2,1,0:T(8,128)(2,1)} %bitcast.24), calls=%async_computation.3 | async-start | bytes 3145728 | tf_op jit(solution)/shard_map/all_to_all | solution.py:290
  126.6 1.6 fusion.5.own_ref
  128.2 35.9 %all-to-all-done.3 = bf16[32,6,32,128]{3,2,1,0:T(8,128)(2,1)S(1)} async-done(((bf16[32,6,32,128]{3,2,1,0:T(8,128)(2,1)}), bf16[32,6,32,128]{3,2,1,0:T(8,128)(2,1)S(1)}, u32[]{:S(2)}, u32[]{:S(2)}) %all-to-all-start.3) | async-done | bytes 1572896 | tf_op jit(solution)/shard_map/all_to_all | solution.py:290
  164.1 1.2 copy-done.1
  165.2 4.3 %shard_map.68 = (f32[14,32,128]{2,1,0:T(8,128)}, bf16[96,32,128]{2,1,0:T(8,128)(2,1)}) custom-call(s32[42]{0:T(128)} %copy-done.3, s32[42]{0:T(128)} %copy-done.4, s32[96]{0:T(128)} %copy-done.5, bf16[192,32,128]{2,1,0:T(8,128)(2,1)} %bitcast.21, f32[14,32,128]{2,1,0:T(8,128)} %fusion.5.own_ref, bf16[14,3,128,128]{3,2,1,0:T(8,128)(2,1)} %c_ref.5), custom_call_target="tpu_custom_call" | custom-call | tf_op jit(solution)/shard_map/pallas_call | solution.py:271
  169.6 24.4 %all_to_all.28 = bf16[32,3,32,128]{3,2,1,0:T(8,128)(2,1)} all-to-all(bf16[32,3,32,128]{3,2,1,0:T(8,128)(2,1)} %bitcast.26), channel_id=1, replica_groups=mesh['rows'=32] {'rows'}, dimensions={0} | all-to-all | bytes 1572864 | tf_op jit(solution)/shard_map/all_to_all | solution.py:290
  194.0 5.9 %shard_map.69 = f32[32,1792]{1,0:T(8,128)} custom-call(s32[42]{0:T(128)} %copy-done.3, s32[42]{0:T(128)} %copy-done.4, bf16[96,32,128]{2,1,0:T(8,128)(2,1)} %bitcast.23, f32[14,32,128]{2,1,0:T(8,128)} %get-tuple-element.23.middle_ref, f32[14,128,128]{2,1,0:T(8,128)} %get-tuple-element.24.k_ref, bf16[14,3,128,128]{3,2,1,0:T(8,128)(2,1)} %get-tuple-element.25.fh_ref, ...), custom_call_target="tpu_custom_call" | custom-call | tf_op jit(solution)/shard_map/pallas_call | solution.py:271
  (25 shorter events, 1.0 us)
Async XLA Ops:
  1.8 10.9 %copy-start.3 = (s32[42]{0:T(128)}, s32[42]{0:T(128)S(1)}, u32[]{:S(2)}) copy-start(s32[42]{0:T(128)S(1)} %reshape.75.target_ref) | copy-start | bytes 508
  2.1 10.6 %copy-start.4 = (s32[42]{0:T(128)}, s32[42]{0:T(128)S(1)}, u32[]{:S(2)}) copy-start(s32[42]{0:T(128)S(1)} %select_reduce_fusion.1.rank_ref) | copy-start | bytes 508
  2.9 20.5 %all-to-all-start = ((s32[32,1,3]{2,1,0:T(1,128)}), s32[32,1,3]{2,1,0:T(1,128)S(1)}, u32[]{:S(2)}, u32[]{:S(2)}) async-start(s32[32,1,3]{2,1,0:T(1,128)} %bitcast), calls=%async_computation | async-start | bytes 32768 | tf_op jit(solution)/shard_map/all_to_all | solution.py:290
  24.7 49.3 %copy-start.5 = (s32[96]{0:T(128)}, s32[96]{0:T(128)S(1)}, u32[]{:S(2)}) copy-start(s32[96]{0:T(128)S(1)} %reshape.76.incoming_ref) | copy-start | bytes 1156
  122.7 3.9 %copy-start = (f32[14,128,128]{2,1,0:T(8,128)S(1)}, f32[14,128,128]{2,1,0:T(8,128)}, u32[]{:S(2)}) copy-start(f32[14,128,128]{2,1,0:T(8,128)} %fusion.1.d_ref) | copy-start | bytes 2752516
  122.7 3.9 %copy-start.2 = (f32[14,32,128]{2,1,0:T(8,128)S(1)}, f32[14,32,128]{2,1,0:T(8,128)}, u32[]{:S(2)}) copy-start(f32[14,32,128]{2,1,0:T(8,128)} %get-tuple-element.21) | copy-start | bytes 688132
  122.7 41.3 %all-to-all-start.3 = ((bf16[32,6,32,128]{3,2,1,0:T(8,128)(2,1)}), bf16[32,6,32,128]{3,2,1,0:T(8,128)(2,1)S(1)}, u32[]{:S(2)}, u32[]{:S(2)}) async-start(bf16[32,6,32,128]{3,2,1,0:T(8,128)(2,1)} %bitcast.24), calls=%async_computation.3 | async-start | bytes 3145728 | tf_op jit(solution)/shard_map/all_to_all | solution.py:290
  164.1 1.2 copy-start.1
